TPU v7x, 32 devices: a whole 2x2x4 slice. The times are simulated.
32 devices in a mesh: team: 4 (over z), blk: 4 (over y, x), head: 2 (over core).
Axes of the slice: x: 2, y: 2, z: 4, core: 2. Of those that a mesh axis runs over, the one named last changes fastest.
Arguments:
- query: bfloat16 [2048, 2560], P(('team', 'blk'), 'head'), parts along dimension 1, may hold values from -15 to 15
- keys: bfloat16 [2048, 2560], P(('team', 'blk'), 'head'), parts along dimension 1, may hold values from -6 to 6
- values: bfloat16 [2048, 2560], P(('team', 'blk'), 'head'), parts along dimension 1, may hold values from -6 to 6
Outputs:
- attended: bfloat16 [2048, 2560], P(('team', 'blk'), 'head'), parts along dimension 1
There are 2 independent parts, one for each index of `head`. A program takes and returns all parts, laid end to end along the dimension named above; each array names one. Nothing has to cross between parts.
All inputs are finite; a program needn't handle non-finite values.
Results may differ from a plain program's by a relative error of at most 0.006.
Values may be sent and summed in bfloat16 or wider, within the bound.
A program may use at most 128 MiB of HBM per device.

v0:
```python
import math
import jax
import jax.numpy as jnp
from jax import lax
from jax.sharding import PartitionSpec as P

HEAD_DIM = 128


def shifted(value, axis, by):
    count = lax.axis_size(axis)
    return lax.ppermute(value, axis, [(i, (i + by) % count) for i in range(count)])


def on_device(query, keys, values):
    shard_rows = query.shape[0]
    feature_width = query.shape[1]
    head_count = feature_width // HEAD_DIM
    score_scale = 1.0 / math.sqrt(HEAD_DIM)
    team_query = lax.all_gather(query, "team", axis=0, tiled=True)
    team_heads = team_query.reshape(-1, head_count, HEAD_DIM)

    def scores_of(key_block):
        key_heads = key_block.reshape(shard_rows, head_count, HEAD_DIM)
        return (
            jnp.einsum("qhd,khd->qhk", team_heads, key_heads, preferred_element_type=jnp.float32)
            * score_scale
        )

    def weighted(weights, value_block):
        value_heads = value_block.reshape(shard_rows, head_count, HEAD_DIM)
        return jnp.einsum(
            "qhk,khd->qhd",
            weights.astype(jnp.bfloat16),
            value_heads,
            preferred_element_type=jnp.float32,
        )

    def absorb(state, key_block, value_block):
        row_peak, row_total, accumulated = state
        scores = scores_of(key_block)
        new_peak = jnp.maximum(row_peak, jnp.max(scores, axis=2))
        rescale = jnp.exp(row_peak - new_peak)
        weights = jnp.exp(scores - new_peak[..., None])
        row_total = row_total * rescale + jnp.sum(weights, axis=2)
        accumulated = accumulated * rescale[..., None] + weighted(weights, value_block)
        return (new_peak, row_total, accumulated)

    first_scores = scores_of(keys)
    first_peak = jnp.max(first_scores, axis=2)
    first_weights = jnp.exp(first_scores - first_peak[..., None])
    state = (first_peak, jnp.sum(first_weights, axis=2), weighted(first_weights, values))

    def step_ahead(key_block, value_block):
        return shifted((key_block, value_block), "blk", 1)

    def step_behind(key_block, value_block):
        return shifted((key_block, value_block), "blk", -1)

    block_count = lax.axis_size("blk")

    def one_turn(turn_index, carried):
        ahead_keys, ahead_values, behind_keys, behind_values, inner = carried
        ahead_keys, ahead_values = step_ahead(ahead_keys, ahead_values)
        behind_keys, behind_values = step_behind(behind_keys, behind_values)
        inner = absorb(inner, ahead_keys, ahead_values)
        inner = absorb(inner, behind_keys, behind_values)
        return (ahead_keys, ahead_values, behind_keys, behind_values, inner)

    carried = lax.fori_loop(0, block_count // 2 - 1, one_turn, (keys, values, keys, values, state))
    last_keys, last_values = step_ahead(carried[0], carried[1])
    row_peak, row_total, accumulated = absorb(carried[4], last_keys, last_values)
    peaks, totals, sums = (
        lax.all_to_all(row_peak[None], "team", split_axis=1, concat_axis=0, tiled=True),
        lax.all_to_all(row_total[None], "team", split_axis=1, concat_axis=0, tiled=True),
        lax.all_to_all(accumulated[None], "team", split_axis=1, concat_axis=0, tiled=True),
    )
    joint_peak = jnp.max(peaks, axis=0)
    rescale = jnp.exp(peaks - joint_peak[None])
    own_total = jnp.sum(totals * rescale, axis=0)
    own_sum = jnp.sum(sums * rescale[..., None], axis=0)
    attended = (own_sum / own_total[..., None]).astype(jnp.bfloat16)
    return attended.reshape(shard_rows, feature_width)


def solution(mesh):
    placed = (P(("team", "blk"), "head"), P(("team", "blk"), "head"), P(("team", "blk"), "head"))
    return jax.shard_map(
        on_device, mesh=mesh, in_specs=placed, out_specs=P(("team", "blk"), "head"), check_vma=False
    )
```

profile of v0, /device:TPU:0, one launch (start us, length us, event | category | flops | bytes accessed | tf_op | source)
XLA Modules:
  0.0 162.7 jit_solution(10376589958835616199)
XLA Ops:
  6.5 0.0 all-gather.2.cloned.1.call-start
  6.5 1.9 %copy.106 = bf16[128,1280]{0,1:T(8,128)(2,1)} copy(bf16[128,1280]{1,0:T(8,128)(2,1)} %param.3) | data formatting | bytes 655360 | tf_op args[0]
  8.4 0.0 all-gather.2.cloned.1.call-update
  8.4 1.2 copy.105
  9.6 3.0 %collective-permute-start = (bf16[128,1280]{0,1:T(8,128)(2,1)S(1)}, bf16[128,1280]{0,1:T(8,128)(2,1)S(1)}, u32[]{:S(2)}, u32[]{:S(2)}) collective-permute-start(bf16[128,1280]{0,1:T(8,128)(2,1)S(1)} %copy.105), channel_id=1, source_target_pairs={{0,2},{2,4},{4,6},{6,0},{1,3},{3,5},{5,7},{7,1},{8,10},{10,12},{12... | collective-permute-start | bytes 983048 | tf_op jit(solution)/shard_map/while/body/eval_jaxpr/ppermute | solution.py:12
  12.6 1.2 copy.109
  13.8 1.5 collective-permute-start.1
  15.4 1.4 collective-permute-start.2
  16.8 0.1 collective-permute-start.3
  16.9 5.2 %collective-permute-done = bf16[128,1280]{0,1:T(8,128)(2,1)S(1)} collective-permute-done((bf16[128,1280]{0,1:T(8,128)(2,1)S(1)}, bf16[128,1280]{0,1:T(8,128)(2,1)S(1)}, u32[]{:S(2)}, u32[]{:S(2)}) %collective-permute-start) | collective-permute-done | bytes 327712 | tf_op jit(solution)/shard_map/while/body/eval_jaxpr/ppermute | solution.py:12
  22.1 1.1 collective-permute-start.4
  23.2 6.1 %collective-permute-done.1 = bf16[128,1280]{0,1:T(8,128)(2,1)} collective-permute-done((bf16[128,1280]{0,1:T(8,128)(2,1)S(1)}, bf16[128,1280]{0,1:T(8,128)(2,1)}, u32[]{:S(2)}, u32[]{:S(2)}) %collective-permute-start.1) | collective-permute-done | bytes 327712 | tf_op jit(solution)/shard_map/while/body/eval_jaxpr/ppermute | solution.py:12
  29.3 1.1 collective-permute-start.5
  30.3 14.8 %all-gather.2.cloned.1.call-done = bf16[512,1280]{0,1:T(8,128)(2,1)} async-done(((bf16[128,1280]{0,1:T(8,128)(2,1)}), bf16[512,1280]{0,1:T(8,128)(2,1)}) %all-gather.2.cloned.1.call-update) | async-done | bytes 1310736 | tf_op jit(solution)/shard_map/all_gather | solution.py:20
  45.1 2.0 %bitcast_reduce_fusion.3 = (f32[512,10]{0,1:T(8,128)S(1)}, f32[10,128,512]{2,1,0:T(8,128)S(1)}) fusion(bf16[128,10,128]{0,2,1:T(8,128)(2,1)S(1)} %bitcast.149, bf16[512,10,128]{0,2,1:T(8,128)(2,1)} %bitcast.142), kind=kOutput, calls=%fused_computation.17 | convolution fusion | flops 169077760 | bytes 4280320 | tf_op jit(solution)/shard_map/qhd,khd->qhk/dot_general | solution.py:26
  47.1 0.0 copy-start
  47.1 0.0 copy-done.5
  47.1 0.6 bitcast_reduce_fusion.2
  47.7 0.0 collective-permute-done.2
  47.7 0.6 bitcast_reduce_fusion.1
  48.3 1.9 %collective-permute-done.4 = bf16[128,1280]{0,1:T(8,128)(2,1)S(1)} collective-permute-done((bf16[128,1280]{0,1:T(8,128)(2,1)S(1)}, bf16[128,1280]{0,1:T(8,128)(2,1)S(1)}, u32[]{:S(2)}, u32[]{:S(2)}) %collective-permute-start.4) | collective-permute-done | bytes 327712 | tf_op jit(solution)/shard_map/ppermute | solution.py:12
  50.2 0.7 copy-done.7
  51.0 1.5 bitcast_reduce_fusion
  52.5 0.6 subtract_exponential_fusion.2
  53.1 0.6 subtract_exponential_fusion.1
  53.8 0.6 subtract_exponential_fusion
  54.4 0.5 fusion.11
  54.9 1.0 fusion.7
  55.9 0.5 fusion.13
  56.3 0.6 bitcast_maximum_fusion
  57.0 0.1 copy.130
  57.1 0.6 broadcast.52
  57.7 1.3 reduce.2
  59.0 0.8 reshape.207
  59.8 5.3 %all-to-all-start.1 = ((f32[4,1,1280]{2,1,0:T(1,128)}), f32[4,1,1280]{2,1,0:T(1,128)S(1)}, u32[]{:S(2)}, u32[]{:S(2)}) async-start(f32[4,1,1280]{2,1,0:T(1,128)} %reshape.207), calls=%async_computation.1 | async-start | bytes 40960 | tf_op jit(solution)/shard_map/all_to_all | solution.py:74
  65.1 0.0 collective-permute-done.3
  65.1 4.2 %fusion.16 = f32[10,512,128]{2,1,0:T(8,128)} fusion(bf16[128,10,128]{0,2,1:T(8,128)(2,1)} %bitcast.11, f32[10,128,512]{2,1,0:T(8,128)} %copy-done.4, f32[512,10]{0,1:T(8,128)} %copy-done.6), kind=kOutput, calls=%fused_computation.28 | convolution fusion | flops 169738240 | bytes 5591040 | tf_op jit(solution)/shard_map/while/body/eval_jaxpr/qhk,khd->qhd/dot_general | solution.py:32
  69.3 0.0 copy-done.3
  69.3 3.3 %fusion.18 = f32[10,512,128]{2,1,0:T(8,128)} fusion(bf16[128,10,128]{0,2,1:T(8,128)(2,1)} %bitcast.7, f32[10,128,512]{2,1,0:T(8,128)S(1)} %copy-done.3, f32[512,10]{0,1:T(8,128)S(1)} %get-tuple-element.24), kind=kOutput, calls=%fused_computation.29 | convolution fusion | flops 169738240 | bytes 5591040 | tf_op jit(solution)/shard_map/while/body/eval_jaxpr/qhk,khd->qhd/dot_general | solution.py:32
  72.7 2.2 %fusion.20 = f32[10,512,128]{2,1,0:T(8,128)} fusion(bf16[128,10,128]{0,2,1:T(8,128)(2,1)S(1)} %bitcast.151, f32[10,128,512]{2,1,0:T(8,128)S(1)} %copy-done.1, f32[512,10]{0,1:T(8,128)S(1)} %get-tuple-element.42), kind=kOutput, calls=%fused_computation.30 | convolution fusion | flops 169738240 | bytes 5591040 | tf_op jit(solution)/shard_map/qhk,khd->qhd/dot_general | solution.py:32
  74.9 0.0 copy-done.13
  74.9 0.1 copy.132
  75.0 1.3 reduce
  76.3 0.8 reshape.209
  77.1 0.0 all-to-all-done.1
  77.1 5.1 %all-to-all-start.2 = ((f32[4,1,1280]{2,1,0:T(1,128)}), f32[4,1,1280]{2,1,0:T(1,128)S(1)}, u32[]{:S(2)}, u32[]{:S(2)}) async-start(f32[4,1,1280]{2,1,0:T(1,128)} %reshape.209), calls=%async_computation.2 | async-start | bytes 40960 | tf_op jit(solution)/shard_map/all_to_all | solution.py:75
  82.2 0.0 collective-permute-done.5
  82.2 5.5 %fusion = f32[1,512,10,128]{3,1,2,0:T(8,128)S(1)} fusion(f32[10,512,128]{2,1,0:T(8,128)} %fusion.16, f32[10,512,128]{2,1,0:T(8,128)} %fusion.18, f32[10,512,128]{2,1,0:T(8,128)} %fusion.20, bf16[128,10,128]{0,2,1:T(8,128)(2,1)} %bitcast.15, f32[10,128,512]{2,1,0:T(8,128)S(1)} %get-tuple-element.49, f32[512,10]{0,1:T(8,128)S(1)} %copy-done.9, ...), kind=kOutput, calls=%fused_computation.1 | convolution fusion | flops 173670400 | bytes 13516800 | tf_op jit(solution)/shard_map/qhk,khd->qhd/dot_general | solution.py:32
  87.7 4.2 %copy.128 = f32[1,512,10,128]{3,0,2,1:T(1,128)} copy(f32[1,512,10,128]{3,1,2,0:T(8,128)S(1)} %fusion) | data formatting | bytes 5242880 | tf_op jit(solution)/shard_map/broadcast_in_dim | solution.py:76
  91.9 0.0 all-to-all-done.2
  92.0 5.1 %all-to-all-start = ((f32[1,512,10,128]{3,0,2,1:T(1,128)}), f32[1,512,10,128]{3,0,2,1:T(1,128)S(1)}, u32[]{:S(2)}, u32[]{:S(2)}) async-start(f32[1,512,10,128]{3,0,2,1:T(1,128)} %copy.128), calls=%async_computation | async-start | bytes 5242880 | tf_op jit(solution)/shard_map/all_to_all | solution.py:76
  97.0 0.7 reduce.3
  97.7 0.4 reshape.208
  98.1 0.1 copy.152
  98.3 0.1 copy.154
  98.3 0.7 reduce.1
  99.0 0.4 reshape.210
  99.4 0.1 copy.153
  99.6 53.8 %all-to-all-done = f32[1,512,10,128]{3,0,2,1:T(1,128)S(1)} async-done(((f32[1,512,10,128]{3,0,2,1:T(1,128)}), f32[1,512,10,128]{3,0,2,1:T(1,128)S(1)}, u32[]{:S(2)}, u32[]{:S(2)}) %all-to-all-start) | async-done | bytes 2621472 | tf_op jit(solution)/shard_map/all_to_all | solution.py:76
  153.4 0.2 copy.129
  153.6 0.9 multiply_reduce_fusion
  154.5 0.2 divide_convert_fusion
  154.7 0.2 copy.134
  154.9 0.9 copy.135
  (25 shorter events, 0.1 us)
Async XLA Ops:
  6.5 38.6 %all-gather.2.cloned.1.call-start = ((), (), s32[]{:S(2)}) async-start(), calls=%async_computation.3 | async-start | bytes 1638400 | tf_op jit(solution)/shard_map/all_gather | solution.py:20
  9.6 12.5 %collective-permute-start = (bf16[128,1280]{0,1:T(8,128)(2,1)S(1)}, bf16[128,1280]{0,1:T(8,128)(2,1)S(1)}, u32[]{:S(2)}, u32[]{:S(2)}) collective-permute-start(bf16[128,1280]{0,1:T(8,128)(2,1)S(1)} %copy.105), channel_id=1, source_target_pairs={{0,2},{2,4},{4,6},{6,0},{1,3},{3,5},{5,7},{7,1},{8,10},{10,12},{12... | collective-permute-start | bytes 983048 | tf_op jit(solution)/shard_map/while/body/eval_jaxpr/ppermute | solution.py:12
  13.8 15.5 %collective-permute-start.1 = (bf16[128,1280]{0,1:T(8,128)(2,1)S(1)}, bf16[128,1280]{0,1:T(8,128)(2,1)}, u32[]{:S(2)}, u32[]{:S(2)}) collective-permute-start(bf16[128,1280]{0,1:T(8,128)(2,1)S(1)} %copy.109), channel_id=1, source_target_pairs={{0,2},{2,4},{4,6},{6,0},{1,3},{3,5},{5,7},{7,1},{8,10},{10,12},{12... | collective-permute-start | bytes 983048 | tf_op jit(solution)/shard_map/while/body/eval_jaxpr/ppermute | solution.py:12
  15.4 32.4 %collective-permute-start.2 = (bf16[128,1280]{0,1:T(8,128)(2,1)S(1)}, bf16[128,1280]{0,1:T(8,128)(2,1)S(1)}, u32[]{:S(2)}, u32[]{:S(2)}) collective-permute-start(bf16[128,1280]{0,1:T(8,128)(2,1)S(1)} %copy.105), channel_id=1, source_target_pairs={{0,6},{2,0},{4,2},{6,4},{1,7},{3,1},{5,3},{7,5},{8,14},{10,8},{12,... | collective-permute-start | bytes 983048 | tf_op jit(solution)/shard_map/while/body/eval_jaxpr/ppermute | solution.py:12
  16.8 48.3 %collective-permute-start.3 = (bf16[128,1280]{0,1:T(8,128)(2,1)S(1)}, bf16[128,1280]{0,1:T(8,128)(2,1)}, u32[]{:S(2)}, u32[]{:S(2)}) collective-permute-start(bf16[128,1280]{0,1:T(8,128)(2,1)S(1)} %copy.109), channel_id=1, source_target_pairs={{0,6},{2,0},{4,2},{6,4},{1,7},{3,1},{5,3},{7,5},{8,14},{10,8},{12,... | collective-permute-start | bytes 983048 | tf_op jit(solution)/shard_map/while/body/eval_jaxpr/ppermute | solution.py:12
  22.1 28.1 %collective-permute-start.4 = (bf16[128,1280]{0,1:T(8,128)(2,1)S(1)}, bf16[128,1280]{0,1:T(8,128)(2,1)S(1)}, u32[]{:S(2)}, u32[]{:S(2)}) collective-permute-start(bf16[128,1280]{0,1:T(8,128)(2,1)S(1)} %collective-permute-done), channel_id=1, source_target_pairs={{0,2},{2,4},{4,6},{6,0},{1,3},{3,5},{5,7},{7,1},{8,10},{10,12},{12... | collective-permute-start | bytes 983048 | tf_op jit(solution)/shard_map/ppermute | solution.py:12
  29.3 52.9 %collective-permute-start.5 = (bf16[128,1280]{0,1:T(8,128)(2,1)}, bf16[128,1280]{0,1:T(8,128)(2,1)}, u32[]{:S(2)}, u32[]{:S(2)}) collective-permute-start(bf16[128,1280]{0,1:T(8,128)(2,1)} %collective-permute-done.1), channel_id=1, source_target_pairs={{0,2},{2,4},{4,6},{6,0},{1,3},{3,5},{5,7},{7,1},{8,10},{10,12},{12... | collective-permute-start | bytes 983048 | tf_op jit(solution)/shard_map/ppermute | solution.py:12
  45.1 2.0 %copy-start.5 = (bf16[512,1280]{0,1:T(8,128)(2,1)S(1)}, bf16[512,1280]{0,1:T(8,128)(2,1)}, u32[]{:S(2)}) copy-start(bf16[512,1280]{0,1:T(8,128)(2,1)} %all-gather.2.cloned.1.call-done) | copy-start | bytes 3932164
  47.1 7.8 %copy-start = (f32[10,128,512]{2,1,0:T(8,128)}, f32[10,128,512]{2,1,0:T(8,128)S(1)}, u32[]{:S(2)}) copy-start(f32[10,128,512]{2,1,0:T(8,128)S(1)} %get-tuple-element.43) | copy-start | bytes 7864324
  47.7 7.2 %copy-start.2 = (f32[10,128,512]{2,1,0:T(8,128)}, f32[10,128,512]{2,1,0:T(8,128)S(1)}, u32[]{:S(2)}) copy-start(f32[10,128,512]{2,1,0:T(8,128)S(1)} %get-tuple-element.45) | copy-start | bytes 7864324
  48.3 6.5 %copy-start.4 = (f32[10,128,512]{2,1,0:T(8,128)}, f32[10,128,512]{2,1,0:T(8,128)S(1)}, u32[]{:S(2)}) copy-start(f32[10,128,512]{2,1,0:T(8,128)S(1)} %get-tuple-element.47) | copy-start | bytes 7864324
  50.2 0.7 copy-start.7
  53.8 2.1 %copy-start.6 = (f32[512,10]{0,1:T(8,128)}, f32[512,10]{0,1:T(8,128)S(1)}, u32[]{:S(2)}) copy-start(f32[512,10]{0,1:T(8,128)S(1)} %get-tuple-element.26) | copy-start | bytes 61444
  54.4 1.5 copy-start.8
  59.8 17.3 %all-to-all-start.1 = ((f32[4,1,1280]{2,1,0:T(1,128)}), f32[4,1,1280]{2,1,0:T(1,128)S(1)}, u32[]{:S(2)}, u32[]{:S(2)}) async-start(f32[4,1,1280]{2,1,0:T(1,128)} %reshape.207), calls=%async_computation.1 | async-start | bytes 40960 | tf_op jit(solution)/shard_map/all_to_all | solution.py:74
  65.1 4.2 %copy-start.3 = (f32[10,128,512]{2,1,0:T(8,128)S(1)}, f32[10,128,512]{2,1,0:T(8,128)}, u32[]{:S(2)}) copy-start(f32[10,128,512]{2,1,0:T(8,128)} %copy-done.2) | copy-start | bytes 7864324
  69.3 3.3 %copy-start.1 = (f32[10,128,512]{2,1,0:T(8,128)S(1)}, f32[10,128,512]{2,1,0:T(8,128)}, u32[]{:S(2)}) copy-start(f32[10,128,512]{2,1,0:T(8,128)} %copy-done) | copy-start | bytes 7864324
  72.6 2.3 %copy-start.13 = (f32[1,512,10]{1,2,0:T(8,128)S(1)}, f32[1,512,10]{1,2,0:T(8,128)}, u32[]{:S(2)}) copy-start(f32[1,512,10]{1,2,0:T(8,128)} %get-tuple-element.41) | copy-start | bytes 61444
  72.6 9.6 %copy-start.9 = (f32[512,10]{0,1:T(8,128)S(1)}, f32[512,10]{0,1:T(8,128)}, u32[]{:S(2)}) copy-start(f32[512,10]{0,1:T(8,128)} %copy-done.8) | copy-start | bytes 61444
  72.6 9.6 %copy-start.10 = (f32[512,10]{0,1:T(8,128)S(1)}, f32[512,10]{0,1:T(8,128)}, u32[]{:S(2)}) copy-start(f32[512,10]{0,1:T(8,128)} %get-tuple-element.23) | copy-start | bytes 61444
  72.6 9.6 %copy-start.11 = (f32[512,10]{0,1:T(8,128)S(1)}, f32[512,10]{0,1:T(8,128)}, u32[]{:S(2)}) copy-start(f32[512,10]{0,1:T(8,128)} %get-tuple-element.25) | copy-start | bytes 61444
  72.6 9.6 %copy-start.12 = (f32[512,10]{0,1:T(8,128)S(1)}, f32[512,10]{0,1:T(8,128)}, u32[]{:S(2)}) copy-start(f32[512,10]{0,1:T(8,128)} %get-tuple-element.36) | copy-start | bytes 61444
  77.1 14.8 %all-to-all-start.2 = ((f32[4,1,1280]{2,1,0:T(1,128)}), f32[4,1,1280]{2,1,0:T(1,128)S(1)}, u32[]{:S(2)}, u32[]{:S(2)}) async-start(f32[4,1,1280]{2,1,0:T(1,128)} %reshape.209), calls=%async_computation.2 | async-start | bytes 40960 | tf_op jit(solution)/shard_map/all_to_all | solution.py:75
  92.0 61.4 %all-to-all-start = ((f32[1,512,10,128]{3,0,2,1:T(1,128)}), f32[1,512,10,128]{3,0,2,1:T(1,128)S(1)}, u32[]{:S(2)}, u32[]{:S(2)}) async-start(f32[1,512,10,128]{3,0,2,1:T(1,128)} %copy.128), calls=%async_computation | async-start | bytes 5242880 | tf_op jit(solution)/shard_map/all_to_all | solution.py:76
Sparse Core Ops, SparseCore 0:
  8.9 36.1 all-gather.1
where the time goes:
time: 163 us
  waiting for transfers between devices  81.8 us (50%)
  starting transfers between devices  23.8 us (15%)
  matrix products  19.9 us (12%)
  local copies, waits for them, and re-layouts  14 us (9%)
  between operations  13.7 us (8%)
  other arithmetic  9.52 us (6%)
    all_to_all x1, waiting for transfers between devices, on_device(): lax.all_to_all(accumulated[None], 'team', split_axis=1, concat_axis=0, ti...  53.8 us
    dot_general x4, matrix products, weighted(): jnp.einsum('qhk,khd->qhd', weights.astype(jnp.bfloat16), value_heads, pre...  15.2 us
    all_gather x1, waiting for transfers between devices, on_device(): team_query = lax.all_gather(query, 'team', axis=0, tiled=True)  14.8 us
    ppermute x6, waiting for transfers between devices, shifted(): lax.ppermute(value, axis, [(i, (i + by) % count) for i in range(count)])  13.2 us
    ppermute x6, starting transfers between devices, shifted(): lax.ppermute(value, axis, [(i, (i + by) % count) for i in range(count)])  8.25 us
    unnamed x37, local copies, waits for them, and re-layouts  8.02 us
    all_to_all x1, starting transfers between devices, on_device(): lax.all_to_all(row_peak[None], 'team', split_axis=1, concat_axis=0, tiled...  5.34 us
    all_to_all x1, starting transfers between devices, on_device(): lax.all_to_all(row_total[None], 'team', split_axis=1, concat_axis=0, tile...  5.09 us
  transfers between devices with their start and end apart: 10, of which 5 were waited for; matrix products, arithmetic and copies ran while one was open for 24% of the time, Pallas kernels for 0%

commit v1 on v0

--- a/solution.py
+++ b/solution.py
@@ -3,6 +3,7 @@
 import jax.numpy as jnp
 from jax import lax
 from jax.sharding import PartitionSpec as P
+from jax.lax import axis_index, ppermute, psum
 
 HEAD_DIM = 128
 
@@ -17,7 +18,23 @@
     feature_width = query.shape[1]
     head_count = feature_width // HEAD_DIM
     score_scale = 1.0 / math.sqrt(HEAD_DIM)
-    team_query = lax.all_gather(query, "team", axis=0, tiled=True)
+
+    def enter_slabs(mine_x, axis_key, dim_k):
+        p_count = psum(1, axis_name=axis_key)
+        history = []
+        for b in [*range(1, p_count)]:
+            history.append((b - 1, b))
+        later = history + [(p_count - 1, 0)]
+        built = mine_x
+        vals = [built]
+        for _ in tuple(range(p_count - 1)):
+            built = ppermute(built, axis_name=axis_key, perm=later)
+            vals += [built]
+        local_now = jnp.concatenate([*reversed(vals)], dim_k)
+        all_values = axis_index(axis_key)
+        return jnp.roll(local_now, (all_values + 1) * built.shape[dim_k], axis=dim_k)
+
+    team_query = enter_slabs(query, axis_key="team", dim_k=0)
     team_heads = team_query.reshape(-1, head_count, HEAD_DIM)
 
     def scores_of(key_block):

time: 163 us -> 158 us (0.969)
  between operations: 13.7 us -> 0.36 us
  waiting for transfers between devices: 81.8 us -> 89.5 us
  starting transfers between devices: 23.8 us -> 26.3 us
    ppermute x0 -> x3, waiting for transfers between devices: none -> 15 us  [enter_slabs(): built = ppermute(built, axis_name=axis_key, perm=later)]
    all_gather x1 -> x0, waiting for transfers between devices: 14.8 us -> none  [on_device(): team_query = lax.all_gather(query, 'team', axis=0, tiled=True)]
    ppermute x6, waiting for transfers between devices: 13.2 us -> 22.4 us  [shifted(): lax.ppermute(value, axis, [(i, (i + by) % count) for i in range(count)])]
    ppermute x0 -> x3, starting transfers between devices: none -> 3.11 us  [enter_slabs(): built = ppermute(built, axis_name=axis_key, perm=later)]
    dot_general x4, matrix products: 4.68 us -> 2.29 us  [scores_of(): jnp.einsum('qhd,khd->qhk', team_heads, key_heads, preferred_element_type=...]
    all_to_all x1, waiting for transfers between devices: 53.8 us -> 52.1 us  [on_device(): lax.all_to_all(accumulated[None], 'team', split_axis=1, concat_axis=0, ti...]
    unnamed x37 -> x42, local copies, waits for them, and re-layouts: 8.02 us -> 7.34 us
  transfers between devices with their start and end apart: 10 -> 12, of which waited for: 5 -> 7; matrix products, arithmetic and copies ran while one was open for 24% -> 24% of each run, Pallas kernels for 0% -> 0%
where the time goes in v1:
time: 158 us
  waiting for transfers between devices  89.5 us (57%)
  starting transfers between devices  26.3 us (17%)
  matrix products  18.5 us (12%)
  local copies, waits for them, and re-layouts  13.6 us (9%)
  other arithmetic  9.52 us (6%)
    all_to_all x1, waiting for transfers between devices, on_device(): lax.all_to_all(accumulated[None], 'team', split_axis=1, concat_axis=0, ti...  52.1 us
    ppermute x6, waiting for transfers between devices, shifted(): lax.ppermute(value, axis, [(i, (i + by) % count) for i in range(count)])  22.4 us
    dot_general x4, matrix products, weighted(): jnp.einsum('qhk,khd->qhd', weights.astype(jnp.bfloat16), value_heads, pre...  16.2 us
    ppermute x3, waiting for transfers between devices, enter_slabs(): built = ppermute(built, axis_name=axis_key, perm=later)  15 us
    ppermute x6, starting transfers between devices, shifted(): lax.ppermute(value, axis, [(i, (i + by) % count) for i in range(count)])  7.93 us
    unnamed x42, local copies, waits for them, and re-layouts  7.34 us
    all_to_all x1, starting transfers between devices, on_device(): lax.all_to_all(row_total[None], 'team', split_axis=1, concat_axis=0, tile...  5.09 us
    all_to_all x1, starting transfers between devices, on_device(): lax.all_to_all(row_peak[None], 'team', split_axis=1, concat_axis=0, tiled...  5.09 us
  transfers between devices with their start and end apart: 12, of which 7 were waited for; matrix products, arithmetic and copies ran while one was open for 24% of the time, Pallas kernels for 0%

profile of v1, /device:TPU:0, one launch (start us, length us, event | category | flops | bytes accessed | tf_op | source)
XLA Modules:
  0.0 157.7 jit_solution(5831001619518844146)
XLA Ops:
  0.0 1.2 copy.111
  1.2 3.1 %collective-permute-start = (bf16[128,1280]{0,1:T(8,128)(2,1)S(1)}, bf16[128,1280]{0,1:T(8,128)(2,1)S(1)}, u32[]{:S(2)}, u32[]{:S(2)}) collective-permute-start(bf16[128,1280]{0,1:T(8,128)(2,1)S(1)} %copy.111), channel_id=1, source_target_pairs={{0,8},{8,16},{16,24},{24,0},{1,9},{9,17},{17,25},{25,1},{2,10},{10... | collective-permute-start | bytes 983048 | tf_op jit(solution)/shard_map/ppermute | solution.py:31
  4.3 9.7 %collective-permute-done = bf16[128,1280]{0,1:T(8,128)(2,1)S(1)} collective-permute-done((bf16[128,1280]{0,1:T(8,128)(2,1)S(1)}, bf16[128,1280]{0,1:T(8,128)(2,1)S(1)}, u32[]{:S(2)}, u32[]{:S(2)}) %collective-permute-start) | collective-permute-done | bytes 327712 | tf_op jit(solution)/shard_map/ppermute | solution.py:31
  14.0 1.2 copy.114
  15.2 1.5 collective-permute-start.3
  16.8 1.2 copy.117
  17.9 1.5 collective-permute-start.4
  19.5 5.2 %collective-permute-done.1 = bf16[128,1280]{0,1:T(8,128)(2,1)S(1)} collective-permute-done((bf16[128,1280]{0,1:T(8,128)(2,1)S(1)}, bf16[128,1280]{0,1:T(8,128)(2,1)S(1)}, u32[]{:S(2)}, u32[]{:S(2)}) %collective-permute-start.1) | collective-permute-done | bytes 327712 | tf_op jit(solution)/shard_map/ppermute | solution.py:31
  24.7 2.2 %collective-permute-start.5 = (bf16[128,1280]{0,1:T(8,128)(2,1)S(1)}, bf16[128,1280]{0,1:T(8,128)(2,1)S(1)}, u32[]{:S(2)}, u32[]{:S(2)}) collective-permute-start(bf16[128,1280]{0,1:T(8,128)(2,1)S(1)} %copy.114), channel_id=1, source_target_pairs={{0,6},{2,0},{4,2},{6,4},{1,7},{3,1},{5,3},{7,5},{8,14},{10,8},{12,... | collective-permute-start | bytes 983048 | tf_op jit(solution)/shard_map/while/body/eval_jaxpr/ppermute | solution.py:13
  26.9 0.5 collective-permute-start.6
  27.5 1.5 collective-permute-start.7
  29.0 4.9 %collective-permute-done.4 = bf16[128,1280]{0,1:T(8,128)(2,1)} collective-permute-done((bf16[128,1280]{0,1:T(8,128)(2,1)S(1)}, bf16[128,1280]{0,1:T(8,128)(2,1)}, u32[]{:S(2)}, u32[]{:S(2)}) %collective-permute-start.4) | collective-permute-done | bytes 327712 | tf_op jit(solution)/shard_map/while/body/eval_jaxpr/ppermute | solution.py:13
  33.9 0.6 collective-permute-start.8
  34.5 0.1 collective-permute-done.2
  34.5 0.1 constant_dynamic-update-slice_fusion.7
  34.6 0.1 constant_dynamic-update-slice_fusion.6
  34.7 0.1 constant_dynamic-update-slice_fusion.5
  34.8 0.1 constant_dynamic-update-slice_fusion.4
  35.0 0.1 constant_dynamic-update-slice_fusion.3
  35.1 0.1 constant_dynamic-update-slice_fusion.2
  35.2 0.1 constant_dynamic-update-slice_fusion.1
  35.3 0.1 constant_dynamic-update-slice_fusion
  35.4 0.1 constant_dynamic-slice_fusion
  35.6 0.6 bitcast_reduce_fusion.2
  36.2 0.6 bitcast_reduce_fusion.3
  36.8 4.1 %collective-permute-done.5 = bf16[128,1280]{0,1:T(8,128)(2,1)S(1)} collective-permute-done((bf16[128,1280]{0,1:T(8,128)(2,1)S(1)}, bf16[128,1280]{0,1:T(8,128)(2,1)S(1)}, u32[]{:S(2)}, u32[]{:S(2)}) %collective-permute-start.5) | collective-permute-done | bytes 327712 | tf_op jit(solution)/shard_map/while/body/eval_jaxpr/ppermute | solution.py:13
  40.8 0.6 bitcast_reduce_fusion.1
  41.4 13.4 %collective-permute-done.7 = bf16[128,1280]{0,1:T(8,128)(2,1)S(1)} collective-permute-done((bf16[128,1280]{0,1:T(8,128)(2,1)S(1)}, bf16[128,1280]{0,1:T(8,128)(2,1)S(1)}, u32[]{:S(2)}, u32[]{:S(2)}) %collective-permute-start.7) | collective-permute-done | bytes 327712 | tf_op jit(solution)/shard_map/ppermute | solution.py:13
  54.8 0.6 bitcast_reduce_fusion
  55.4 0.6 subtract_exponential_fusion.2
  56.0 0.6 subtract_exponential_fusion.1
  56.6 0.5 fusion.11
  57.1 0.6 subtract_exponential_fusion
  57.7 1.0 fusion.7
  58.7 0.5 fusion.13
  59.2 0.6 bitcast_maximum_fusion
  59.8 0.1 copy.138
  60.0 0.6 broadcast.53
  60.6 1.3 reduce.2
  61.8 0.8 reshape.207
  62.6 5.1 %all-to-all-start.1 = ((f32[4,1,1280]{2,1,0:T(1,128)}), f32[4,1,1280]{2,1,0:T(1,128)S(1)}, u32[]{:S(2)}, u32[]{:S(2)}) async-start(f32[4,1,1280]{2,1,0:T(1,128)} %reshape.207), calls=%async_computation.1 | async-start | bytes 40960 | tf_op jit(solution)/shard_map/all_to_all | solution.py:91
  67.7 4.1 %fusion.20 = f32[10,512,128]{2,1,0:T(8,128)} fusion(bf16[128,10,128]{0,2,1:T(8,128)(2,1)S(1)} %bitcast.151, f32[10,512,128]{1,2,0:T(8,128)} %copy-done.4, f32[512,10]{0,1:T(8,128)S(1)} %get-tuple-element.42), kind=kOutput, calls=%fused_computation.30 | convolution fusion | flops 169738240 | bytes 5591040 | tf_op jit(solution)/shard_map/qhk,khd->qhd/dot_general | solution.py:49
  71.8 3.3 %fusion.18 = f32[10,512,128]{2,1,0:T(8,128)} fusion(bf16[128,10,128]{0,2,1:T(8,128)(2,1)} %bitcast.7, f32[10,512,128]{1,2,0:T(8,128)S(1)} %copy-done.1, f32[512,10]{0,1:T(8,128)S(1)} %copy-done.6), kind=kOutput, calls=%fused_computation.29 | convolution fusion | flops 169738240 | bytes 5591040 | tf_op jit(solution)/shard_map/while/body/eval_jaxpr/qhk,khd->qhd/dot_general | solution.py:49
  75.2 3.2 %fusion.16 = f32[10,512,128]{2,1,0:T(8,128)} fusion(bf16[128,10,128]{0,2,1:T(8,128)(2,1)} %bitcast.11, f32[10,512,128]{1,2,0:T(8,128)S(1)} %copy-done.3, f32[512,10]{0,1:T(8,128)S(1)} %get-tuple-element.26), kind=kOutput, calls=%fused_computation.28 | convolution fusion | flops 169738240 | bytes 5591040 | tf_op jit(solution)/shard_map/while/body/eval_jaxpr/qhk,khd->qhd/dot_general | solution.py:49
  78.5 0.1 copy.140
  78.6 1.3 reduce
  79.9 0.8 reshape.209
  80.7 5.1 %all-to-all-start.2 = ((f32[4,1,1280]{2,1,0:T(1,128)}), f32[4,1,1280]{2,1,0:T(1,128)S(1)}, u32[]{:S(2)}, u32[]{:S(2)}) async-start(f32[4,1,1280]{2,1,0:T(1,128)} %reshape.209), calls=%async_computation.2 | async-start | bytes 40960 | tf_op jit(solution)/shard_map/all_to_all | solution.py:92
  85.8 5.5 %fusion = f32[1,512,10,128]{3,1,2,0:T(8,128)S(1)} fusion(f32[10,512,128]{2,1,0:T(8,128)} %fusion.16, f32[10,512,128]{2,1,0:T(8,128)} %fusion.18, f32[10,512,128]{2,1,0:T(8,128)} %fusion.20, bf16[128,10,128]{0,2,1:T(8,128)(2,1)} %bitcast.15, f32[10,512,128]{1,2,0:T(8,128)S(1)} %get-tuple-element.49, f32[512,10]{0,1:T(8,128)S(1)} %copy-done.8, ...), kind=kOutput, calls=%fused_computation.1 | convolution fusion | flops 173670400 | bytes 13516800 | tf_op jit(solution)/shard_map/qhk,khd->qhd/dot_general | solution.py:49
  91.3 4.2 %copy.136 = f32[1,512,10,128]{3,0,2,1:T(1,128)} copy(f32[1,512,10,128]{3,1,2,0:T(8,128)S(1)} %fusion) | data formatting | bytes 5242880 | tf_op jit(solution)/shard_map/broadcast_in_dim | solution.py:93
  95.5 5.1 %all-to-all-start = ((f32[1,512,10,128]{3,0,2,1:T(1,128)}), f32[1,512,10,128]{3,0,2,1:T(1,128)S(1)}, u32[]{:S(2)}, u32[]{:S(2)}) async-start(f32[1,512,10,128]{3,0,2,1:T(1,128)} %copy.136), calls=%async_computation | async-start | bytes 5242880 | tf_op jit(solution)/shard_map/all_to_all | solution.py:93
  100.6 0.7 reduce.3
  101.3 0.4 reshape.208
  101.7 0.1 copy.160
  101.9 0.1 copy.162
  101.9 0.7 reduce.1
  102.6 0.4 reshape.210
  103.0 0.1 copy.161
  103.2 52.1 %all-to-all-done = f32[1,512,10,128]{3,0,2,1:T(1,128)S(1)} async-done(((f32[1,512,10,128]{3,0,2,1:T(1,128)}), f32[1,512,10,128]{3,0,2,1:T(1,128)S(1)}, u32[]{:S(2)}, u32[]{:S(2)}) %all-to-all-start) | async-done | bytes 2621472 | tf_op jit(solution)/shard_map/all_to_all | solution.py:93
  155.2 0.2 copy.137
  155.5 0.9 multiply_reduce_fusion
  156.3 0.2 divide_convert_fusion
  156.6 0.2 copy.142
  156.8 0.9 copy.143
  (35 shorter events, 0.1 us)
Async XLA Ops:
  1.2 12.8 %collective-permute-start = (bf16[128,1280]{0,1:T(8,128)(2,1)S(1)}, bf16[128,1280]{0,1:T(8,128)(2,1)S(1)}, u32[]{:S(2)}, u32[]{:S(2)}) collective-permute-start(bf16[128,1280]{0,1:T(8,128)(2,1)S(1)} %copy.111), channel_id=1, source_target_pairs={{0,8},{8,16},{16,24},{24,0},{1,9},{9,17},{17,25},{25,1},{2,10},{10... | collective-permute-start | bytes 983048 | tf_op jit(solution)/shard_map/ppermute | solution.py:31
  14.0 10.7 %collective-permute-start.1 = (bf16[128,1280]{0,1:T(8,128)(2,1)S(1)}, bf16[128,1280]{0,1:T(8,128)(2,1)S(1)}, u32[]{:S(2)}, u32[]{:S(2)}) collective-permute-start(bf16[128,1280]{0,1:T(8,128)(2,1)S(1)} %collective-permute-done), channel_id=1, source_target_pairs={{0,8},{8,16},{16,24},{24,0},{1,9},{9,17},{17,25},{25,1},{2,10},{10... | collective-permute-start | bytes 983048 | tf_op jit(solution)/shard_map/ppermute | solution.py:31
  15.2 12.3 %collective-permute-start.3 = (bf16[128,1280]{0,1:T(8,128)(2,1)S(1)}, bf16[128,1280]{0,1:T(8,128)(2,1)S(1)}, u32[]{:S(2)}, u32[]{:S(2)}) collective-permute-start(bf16[128,1280]{0,1:T(8,128)(2,1)S(1)} %copy.114), channel_id=1, source_target_pairs={{0,2},{2,4},{4,6},{6,0},{1,3},{3,5},{5,7},{7,1},{8,10},{10,12},{12... | collective-permute-start | bytes 983048 | tf_op jit(solution)/shard_map/while/body/eval_jaxpr/ppermute | solution.py:13
  17.9 15.9 %collective-permute-start.4 = (bf16[128,1280]{0,1:T(8,128)(2,1)S(1)}, bf16[128,1280]{0,1:T(8,128)(2,1)}, u32[]{:S(2)}, u32[]{:S(2)}) collective-permute-start(bf16[128,1280]{0,1:T(8,128)(2,1)S(1)} %copy.117), channel_id=1, source_target_pairs={{0,2},{2,4},{4,6},{6,0},{1,3},{3,5},{5,7},{7,1},{8,10},{10,12},{12... | collective-permute-start | bytes 983048 | tf_op jit(solution)/shard_map/while/body/eval_jaxpr/ppermute | solution.py:13
  24.7 9.8 %collective-permute-start.2 = (bf16[128,1280]{0,1:T(8,128)(2,1)S(1)}, bf16[128,1280]{0,1:T(8,128)(2,1)S(1)}, u32[]{:S(2)}, u32[]{:S(2)}) collective-permute-start(bf16[128,1280]{0,1:T(8,128)(2,1)S(1)} %collective-permute-done.1), channel_id=1, source_target_pairs={{0,8},{8,16},{16,24},{24,0},{1,9},{9,17},{17,25},{25,1},{2,10},{10... | collective-permute-start | bytes 983048 | tf_op jit(solution)/shard_map/ppermute | solution.py:31
  24.7 16.1 %collective-permute-start.5 = (bf16[128,1280]{0,1:T(8,128)(2,1)S(1)}, bf16[128,1280]{0,1:T(8,128)(2,1)S(1)}, u32[]{:S(2)}, u32[]{:S(2)}) collective-permute-start(bf16[128,1280]{0,1:T(8,128)(2,1)S(1)} %copy.114), channel_id=1, source_target_pairs={{0,6},{2,0},{4,2},{6,4},{1,7},{3,1},{5,3},{7,5},{8,14},{10,8},{12,... | collective-permute-start | bytes 983048 | tf_op jit(solution)/shard_map/while/body/eval_jaxpr/ppermute | solution.py:13
  26.9 48.2 %collective-permute-start.6 = (bf16[128,1280]{0,1:T(8,128)(2,1)S(1)}, bf16[128,1280]{0,1:T(8,128)(2,1)}, u32[]{:S(2)}, u32[]{:S(2)}) collective-permute-start(bf16[128,1280]{0,1:T(8,128)(2,1)S(1)} %copy.117), channel_id=1, source_target_pairs={{0,6},{2,0},{4,2},{6,4},{1,7},{3,1},{5,3},{7,5},{8,14},{10,8},{12,... | collective-permute-start | bytes 983048 | tf_op jit(solution)/shard_map/while/body/eval_jaxpr/ppermute | solution.py:13
  27.5 27.4 %collective-permute-start.7 = (bf16[128,1280]{0,1:T(8,128)(2,1)S(1)}, bf16[128,1280]{0,1:T(8,128)(2,1)S(1)}, u32[]{:S(2)}, u32[]{:S(2)}) collective-permute-start(bf16[128,1280]{0,1:T(8,128)(2,1)S(1)} %collective-permute-done.3), channel_id=1, source_target_pairs={{0,2},{2,4},{4,6},{6,0},{1,3},{3,5},{5,7},{7,1},{8,10},{10,12},{12... | collective-permute-start | bytes 983048 | tf_op jit(solution)/shard_map/ppermute | solution.py:13
  33.9 51.9 %collective-permute-start.8 = (bf16[128,1280]{0,1:T(8,128)(2,1)}, bf16[128,1280]{0,1:T(8,128)(2,1)}, u32[]{:S(2)}, u32[]{:S(2)}) collective-permute-start(bf16[128,1280]{0,1:T(8,128)(2,1)} %collective-permute-done.4), channel_id=1, source_target_pairs={{0,2},{2,4},{4,6},{6,0},{1,3},{3,5},{5,7},{7,1},{8,10},{10,12},{12... | collective-permute-start | bytes 983048 | tf_op jit(solution)/shard_map/ppermute | solution.py:13
  36.2 21.6 %copy-start = (f32[10,512,128]{1,2,0:T(8,128)}, f32[10,512,128]{1,2,0:T(8,128)S(1)}, u32[]{:S(2)}) copy-start(f32[10,512,128]{1,2,0:T(8,128)S(1)} %get-tuple-element.45) | copy-start | bytes 7864324
  36.8 21.0 %copy-start.4 = (f32[10,512,128]{1,2,0:T(8,128)}, f32[10,512,128]{1,2,0:T(8,128)S(1)}, u32[]{:S(2)}) copy-start(f32[10,512,128]{1,2,0:T(8,128)S(1)} %get-tuple-element.43) | copy-start | bytes 7864324
  41.4 15.7 %copy-start.2 = (f32[10,512,128]{1,2,0:T(8,128)}, f32[10,512,128]{1,2,0:T(8,128)S(1)}, u32[]{:S(2)}) copy-start(f32[10,512,128]{1,2,0:T(8,128)S(1)} %get-tuple-element.47) | copy-start | bytes 7864324
  56.0 2.7 %copy-start.5 = (f32[512,10]{0,1:T(8,128)}, f32[512,10]{0,1:T(8,128)S(1)}, u32[]{:S(2)}) copy-start(f32[512,10]{0,1:T(8,128)S(1)} %get-tuple-element.24) | copy-start | bytes 61444
  57.7 1.0 copy-start.7
  62.6 18.1 %all-to-all-start.1 = ((f32[4,1,1280]{2,1,0:T(1,128)}), f32[4,1,1280]{2,1,0:T(1,128)S(1)}, u32[]{:S(2)}, u32[]{:S(2)}) async-start(f32[4,1,1280]{2,1,0:T(1,128)} %reshape.207), calls=%async_computation.1 | async-start | bytes 40960 | tf_op jit(solution)/shard_map/all_to_all | solution.py:91
  67.7 4.1 %copy-start.1 = (f32[10,512,128]{1,2,0:T(8,128)S(1)}, f32[10,512,128]{1,2,0:T(8,128)}, u32[]{:S(2)}) copy-start(f32[10,512,128]{1,2,0:T(8,128)} %copy-done) | copy-start | bytes 7864324
  67.7 4.1 %copy-start.6 = (f32[512,10]{0,1:T(8,128)S(1)}, f32[512,10]{0,1:T(8,128)}, u32[]{:S(2)}) copy-start(f32[512,10]{0,1:T(8,128)} %copy-done.5) | copy-start | bytes 61444
  71.8 3.3 %copy-start.3 = (f32[10,512,128]{1,2,0:T(8,128)S(1)}, f32[10,512,128]{1,2,0:T(8,128)}, u32[]{:S(2)}) copy-start(f32[10,512,128]{1,2,0:T(8,128)} %copy-done.2) | copy-start | bytes 7864324
  75.2 3.3 %copy-start.12 = (f32[1,512,10]{1,2,0:T(8,128)S(1)}, f32[1,512,10]{1,2,0:T(8,128)}, u32[]{:S(2)}) copy-start(f32[1,512,10]{1,2,0:T(8,128)} %get-tuple-element.41) | copy-start | bytes 61444
  75.2 10.6 %copy-start.8 = (f32[512,10]{0,1:T(8,128)S(1)}, f32[512,10]{0,1:T(8,128)}, u32[]{:S(2)}) copy-start(f32[512,10]{0,1:T(8,128)} %copy-done.7) | copy-start | bytes 61444
  75.2 10.6 %copy-start.9 = (f32[512,10]{0,1:T(8,128)S(1)}, f32[512,10]{0,1:T(8,128)}, u32[]{:S(2)}) copy-start(f32[512,10]{0,1:T(8,128)} %get-tuple-element.23) | copy-start | bytes 61444
  75.2 10.6 %copy-start.10 = (f32[512,10]{0,1:T(8,128)S(1)}, f32[512,10]{0,1:T(8,128)}, u32[]{:S(2)}) copy-start(f32[512,10]{0,1:T(8,128)} %get-tuple-element.25) | copy-start | bytes 61444
  75.2 10.6 %copy-start.11 = (f32[512,10]{0,1:T(8,128)S(1)}, f32[512,10]{0,1:T(8,128)}, u32[]{:S(2)}) copy-start(f32[512,10]{0,1:T(8,128)} %get-tuple-element.36) | copy-start | bytes 61444
  80.7 14.8 %all-to-all-start.2 = ((f32[4,1,1280]{2,1,0:T(1,128)}), f32[4,1,1280]{2,1,0:T(1,128)S(1)}, u32[]{:S(2)}, u32[]{:S(2)}) async-start(f32[4,1,1280]{2,1,0:T(1,128)} %reshape.209), calls=%async_computation.2 | async-start | bytes 40960 | tf_op jit(solution)/shard_map/all_to_all | solution.py:92
  95.5 59.7 %all-to-all-start = ((f32[1,512,10,128]{3,0,2,1:T(1,128)}), f32[1,512,10,128]{3,0,2,1:T(1,128)S(1)}, u32[]{:S(2)}, u32[]{:S(2)}) async-start(f32[1,512,10,128]{3,0,2,1:T(1,128)} %copy.136), calls=%async_computation | async-start | bytes 5242880 | tf_op jit(solution)/shard_map/all_to_all | solution.py:93
